TPU v7x, 32 devices: a whole 2x2x4 slice. The times are simulated.
32 devices in a mesh: grp: 4 (over z), dev: 8 (over y, x, core).
Axes of the slice: x: 2, y: 2, z: 4, core: 2. Of those that a mesh axis runs over, the one named last changes fastest.
Arguments:
- inv_factor: bfloat16 [128, 384, 384], P(('grp', 'dev')), may hold values from -8 to 8
- border: bfloat16 [128, 384, 2048], P(('grp', 'dev')), may hold values from -0.107910156 to 0.107910156
- block_rows: int32 [128], P(('grp', 'dev')), may hold values from 96 to 384
- live_count: int32 [32], P(('grp', 'dev')), may hold values from 1 to 4, as said below
- first_section: float32 [2048, 2048], P('dev'), may hold values from -6 to 6
Outputs:
- condensed: bfloat16 [128, 384, 2048], P(('grp', 'dev'))
- schur: float32 [2048, 2048], P('dev')
Inputs may be any that keep to these rules, and one draw needn't show every extreme that they name: `live_count`: every device holds 1 to 4 live scenarios; at least one device holds 4.
All inputs are finite; a program needn't handle non-finite values.
Results may differ from a plain program's by a relative error of at most 0.001.
Values sent between devices are 32-bit elements; how exact they have to be, the bound alone decides.
No kernel may reach another device: no remote copies, remote signals or barrier semaphores. Data moves between devices by JAX's collectives and lax.ppermute only.
A program may use at most 192 MiB of HBM per device.

v0:
```python
import jax
import jax.numpy as jnp
from jax import lax
from jax.sharding import PartitionSpec as P


def condense(inverse, border_piece):
    return jnp.dot(inverse, border_piece, preferred_element_type=jnp.float32).astype(jnp.bfloat16)


def fill_slots(buffer, source_inv, source_border, start_slot, number):

    def fill_one_step(step, current):
        inverse = lax.dynamic_index_in_dim(source_inv, start_slot + step, 0, keepdims=False)
        border_piece = lax.dynamic_index_in_dim(source_border, start_slot + step, 0, keepdims=False)
        return lax.dynamic_update_index_in_dim(
            current, condense(inverse, border_piece), start_slot + step, 0
        )

    return lax.fori_loop(0, number, fill_one_step, buffer)


def accumulate(buffer, number, term_fn, out_shape):

    def accumulate_one_step(step, current):
        piece = lax.dynamic_index_in_dim(buffer, step, 0, keepdims=False)
        return current + term_fn(piece)

    return lax.fori_loop(0, number, accumulate_one_step, jnp.zeros(out_shape, jnp.float32))


def column_product(columns, piece):
    return lax.dot_general(
        columns, piece, (((0,), (0,)), ((), ())), preferred_element_type=jnp.float32
    )


def body(inv_factor, border, block_rows, live_count, first_section):
    slots, rows_block, width = border.shape
    count_own = live_count[0]
    row_ids = lax.broadcasted_iota(jnp.int32, (slots, rows_block, 1), 1)
    masked_inv = jnp.where(
        row_ids < block_rows[:, None, None], inv_factor, jnp.zeros_like(inv_factor)
    )
    empty = jnp.zeros(border.shape, jnp.bfloat16)
    condensed = fill_slots(empty, masked_inv, border, 0, count_own)
    rows_dev = width // lax.axis_size("dev")
    share = lax.psum_scatter(
        accumulate(
            condensed,
            count_own,
            lambda piece: column_product(piece, piece),
            (lax.axis_size("dev") * rows_dev, width),
        ),
        "dev",
        scatter_dimension=0,
        tiled=True,
    )
    summed = lax.psum(share, "grp")
    return (condensed, first_section - summed)


def solution(mesh):
    placed = (
        P(("grp", "dev"), None, None),
        P(("grp", "dev"), None, None),
        P(("grp", "dev")),
        P(("grp", "dev")),
        P("dev", None),
    )
    return jax.shard_map(
        body,
        mesh=mesh,
        in_specs=placed,
        out_specs=(P(("grp", "dev"), None, None), P("dev", None)),
        check_vma=False,
    )
```

profile of v0, /device:TPU:0, one launch (start us, length us, event | category | flops | bytes accessed | tf_op | source)
XLA Modules:
  0.0 324.5 jit_solution(741342491098842194)
XLA Ops:
  7.2 0.0 reduce-scatter.2.cloned.1.call-start
  7.2 0.7 iota_compare_fusion
  7.9 1.5 broadcast_select_fusion
  9.5 3.5 %broadcast_in_dim.22 = bf16[4,384,2048]{2,1,0:T(8,128)(2,1)} broadcast(bf16[]{:T(256)} %constant.29.clone.1), dimensions={} | broadcast | bytes 6291458 | tf_op jit(solution)/shard_map/broadcast_in_dim | solution.py:45
  13.0 4.9 %while.20 = (s32[]{:T(128)}, bf16[4,384,2048]{2,1,0:T(8,128)(2,1)}, s32[]{:T(128)}, bf16[4,384,384]{2,1,0:T(8,128)(2,1)S(1)}, bf16[4,384,2048]{2,1,0:T(8,128)(2,1)}, /*index=5*/s32[]{:T(128)}, s32[]{:T(128)}, s32[]{:T(128)}) while((s32[]{:T(128)}, bf16[4,384,2048]{2,1,0:T(8,128)(2,1)}, s32[]{:T(128)}, bf16[4,384,384]{2,1,0:T(8,128)(2,1)S(1)}, ...), condition=%wide.region_1.2_spmd, body=%wide.region_0.1_spmd.sunk | while | flops 604766208 | bytes 3442303 | solution.py:20
  13.7 3.5 %fusion.16 = bf16[4,384,2048]{2,1,0:T(8,128)(2,1)} fusion(bf16[4,384,2048]{2,1,0:T(8,128)(2,1)} %get-tuple-element.140, s32[]{:T(128)S(6)} %select_n.20, bf16[4,384,2048]{2,1,0:T(8,128)(2,1)} %get-tuple-element.151, bf16[4,384,384]{2,1,0:T(8,128)(2,1)S(1)} %get-tuple-element.150), kind=kOutput, calls=%fused_computation.2.clone.1 | convolution fusion | flops 604766208 | bytes 3442176 | tf_op jit(solution)/shard_map/while/body/dot_general | solution.py:8
  17.9 7.9 %broadcast_in_dim.25 = f32[2048,2048]{1,0:T(8,128)} broadcast(f32[]{:T(128)} %constant.30.clone.1), dimensions={} | broadcast | bytes 16777220 | tf_op jit(solution)/shard_map/broadcast_in_dim | solution.py:29
  25.7 18.3 %while.21 = (s32[]{:T(128)}, f32[2048,2048]{1,0:T(8,128)}, s32[]{:T(128)}, bf16[4,384,2048]{2,1,0:T(8,128)(2,1)}, s32[]{:T(128)}, /*index=5*/s32[]{:T(128)}, s32[]{:T(128)}) while((s32[]{:T(128)}, f32[2048,2048]{1,0:T(8,128)}, s32[]{:T(128)}, bf16[4,384,2048]{2,1,0:T(8,128)(2,1)}, s32[]{:T(128)}, /*index=5*/s32[]{:T(128)}, s32[]{:T(128)}) %tuple.38), condition=%wide.region_3.4_spmd, body=%wide.region_2.3_spmd.sunk | while | flops 3225419776 | bytes 35127416 | solution.py:29
  26.4 17.0 %convolution_add_fusion.2 = f32[2048,2048]{1,0:T(8,128)} fusion(f32[2048,2048]{1,0:T(8,128)} %get-tuple-element.163, bf16[4,384,2048]{2,1,0:T(8,128)(2,1)} %get-tuple-element.172, s32[]{:T(128)S(6)} %select_n.21), kind=kOutput, calls=%fused_computation.8.clone.1 | convolution fusion | flops 3225419776 | bytes 35127300 | tf_op jit(solution)/shard_map/while/body/dot_general | solution.py:33
  44.1 0.0 copy-start
  44.1 0.0 reduce-scatter.2.cloned.1.call-update
  44.1 0.0 all-reduce.2.cloned.1.call-start
  44.2 181.8 %reduce-scatter.2.cloned.1.call-done = f32[256,2048]{1,0:T(8,128)} async-done(((f32[2048,2048]{1,0:T(8,128)}), f32[256,2048]{1,0:T(8,128)}) %reduce-scatter.2.cloned.1.call-update) | async-done | bytes 2097168 | tf_op jit(solution)/shard_map/reduce_scatter | solution.py:48
  226.0 0.0 all-reduce.2.cloned.1.call-update
  226.0 88.5 %all-reduce.2.cloned.1.call-done = f32[256,2048]{1,0:T(8,128)} async-done(((f32[256,2048]{1,0:T(8,128)}), f32[256,2048]{1,0:T(8,128)}) %all-reduce.2.cloned.1.call-update) | async-done | bytes 2097168 | tf_op jit(solution)/shard_map/psum | solution.py:59
  314.5 0.0 copy-done
  314.5 3.2 sub.3
Async XLA Ops:
  7.2 218.8 %reduce-scatter.2.cloned.1.call-start = ((), (), s32[]{:S(2)}) async-start(), calls=%async_computation.1 | async-start | bytes 18874368 | tf_op jit(solution)/shard_map/reduce_scatter | solution.py:48
  44.1 270.4 %copy-start = (f32[256,2048]{1,0:T(8,128)S(1)}, f32[256,2048]{1,0:T(8,128)}, u32[]{:S(2)}) copy-start(f32[256,2048]{1,0:T(8,128)} %param.13) | copy-start | bytes 6291460
  44.1 270.4 %all-reduce.2.cloned.1.call-start = ((), (), s32[]{:S(2)}) async-start(), calls=%async_computation.2 | async-start | bytes 4194304 | tf_op jit(solution)/shard_map/psum | solution.py:59
Sparse Core Ops, SparseCore 0:
  44.2 181.7 reduce-scatter.1
  228.3 86.1 all-reduce.1
where the time goes:
time: 325 us
  waiting for transfers between devices  270 us (83%)
  matrix products  20.6 us (6%)
  between operations  14.1 us (4%)
  local copies, waits for them, and re-layouts  11.4 us (4%)
  other arithmetic  5.43 us (2%)
    reduce_scatter x1, waiting for transfers between devices, body(): lax.psum_scatter(accumulate(condensed, count_own, lambda piece: column_pr...  182 us
    psum x1, waiting for transfers between devices, body(): summed = lax.psum(share, 'grp')  88.5 us
    dot_general x1, matrix products, column_product(): lax.dot_general(columns, piece, (((0,), (0,)), ((), ())), preferred_eleme...  17 us
    broadcast_in_dim x1, local copies, waits for them, and re-layouts, accumulate(): jnp.zeros(out_shape, jnp.float32)  7.86 us
  transfers between devices with their start and end apart: 2, of which 2 were waited for; matrix products, arithmetic and copies ran while one was open for 0% of the time, Pallas kernels for 0%

commit v1 on v0

v1 whole, which is shorter than its diff:
```python
import functools

import jax
import jax.numpy as jnp
from jax import lax
from jax.experimental import pallas as pl
from jax.experimental.pallas import tpu as pltpu
from jax.sharding import PartitionSpec as P


F32 = jnp.float32
ANY = pl.ANY


def power_of_two(n):
    return n >= 2 and n & (n - 1) == 0


def plain_body(inv_factor, border, block_rows, live_count, first_section):
    slots, rows_block, _ = border.shape
    row_ids = lax.broadcasted_iota(jnp.int32, (slots, rows_block, 1), 1)
    slot_ids = lax.broadcasted_iota(jnp.int32, (slots, rows_block, 1), 0)
    keep = (row_ids < block_rows[:, None, None]) & (slot_ids < live_count[0])
    masked = jnp.where(keep, inv_factor, jnp.zeros_like(inv_factor))
    condensed = jnp.einsum(
        "srk,skc->src", masked, border, preferred_element_type=F32
    ).astype(border.dtype)
    flat = condensed.reshape(slots * rows_block, -1)
    partial = lax.dot_general(
        flat, flat, (((0,), (0,)), ((), ())), preferred_element_type=F32
    )
    share = lax.psum_scatter(partial, "dev", scatter_dimension=0, tiled=True)
    return condensed, first_section - lax.psum(share, "grp")


SHARED = "shared"
DIAGONAL = "diagonal"


def heights(block, parts):
    of = {SHARED: block // 4, DIAGONAL: 3 * block // 8}
    return [of.get(part, block // 2) for part in parts]


def dot_turned(left, right):
    return lax.dot_general(
        left, right, (((0,), (0,)), ((), ())), preferred_element_type=F32
    )


def store_piece(wave, refs, info, chip_at, owner_core, half, row, value):
    _, order = wave
    z = half ^ info[1]
    where = []
    for b in order:
        where.append(z if b == "z" else (chip_at >> (b - 1)) & 1)
    sends = owner_core ^ (info[0] & 1)
    for ref, mine in zip(refs, (0, 1)):

        @pl.when(sends == mine)
        def _():
            ref[(*where, pl.ds(row, value.shape[0]), slice(None))] = value


def pair_products(wave, part, refs, info, read, ratio, block):
    chip = info[0] >> 1
    one, two = chip ^ ratio, chip ^ ratio ^ part
    low, high = jnp.minimum(one, two), jnp.maximum(one, two)
    whole = dot_turned(read(low), read(high))
    row = sum(heights(block, wave[0])[: wave[0].index(part)])
    half = block // 2
    for a in range(2):
        for b in range(2):
            at = (low if a == b else high) ^ chip
            for j in range(2):
                top = a * block + j * half
                value = whole[top : top + half, b * block : (b + 1) * block]
                store_piece(wave, refs, info, at, b, j, row, value)


def own_products(waves, refs, info, read, ratio, block):
    at = info[0] >> 1 ^ ratio
    columns = read(at)
    whole = dot_turned(columns, columns)
    half, quarter, eighth = block // 2, block // 4, block // 8
    for wave, pair in zip(waves, refs):
        rows = heights(block, wave[0])
        for part, start in zip(wave[0], [sum(rows[:k]) for k in range(len(rows))]):
            for core in range(2):
                for j in range(2):
                    if part == SHARED:
                        top = core * half + j * quarter
                        value = whole[top : top + quarter, block:]
                        store_piece(wave, pair, info, ratio, core, j, start, value)
                    if part == DIAGONAL:
                        low = core * block
                        top = low + j * quarter
                        value = whole[top : top + quarter, low : low + block]
                        store_piece(wave, pair, info, ratio, core, j, start, value)
                        top = low + half + j * quarter
                        corner = whole[top : top + quarter, low + half : low + block]
                        value = jnp.concatenate([corner[:eighth], corner[eighth:]], 1)
                        store_piece(
                            wave, pair, info, ratio, core, j, start + quarter, value
                        )


def product_steps(waves, chips):
    steps = []
    for wave in waves:
        for part in wave[0]:
            if isinstance(part, int):
                steps += [(part, r) for r in range(chips) if r < r ^ part]
    if any(isinstance(p, str) for w in waves for p in w[0]):
        steps += [(None, r) for r in range(chips)]
    return steps


def run_products(waves, steps, at, refs, info, read, block):
    pairs = [refs[2 * k : 2 * k + 2] for k in range(len(waves))]
    for k, (part, ratio) in enumerate(steps):

        @pl.when(at == k)
        def _():
            if part is None:
                own_products(waves, pairs, info, read, ratio, block)
            else:
                which = [k for k, w in enumerate(waves) if part in w[0]][0]
                pair_products(
                    waves[which], part, pairs[which], info, read, ratio, block
                )


def wave_shapes(waves, block):
    shapes = []
    for parts, order in waves:
        shape = (2,) * len(order) + (sum(heights(block, parts)), block)
        shapes += [jax.ShapeDtypeStruct(shape, F32)] * 2
    return shapes


def whole_block(shape):
    return pl.BlockSpec(shape, lambda *_: (0,) * len(shape))


def condense_kernel(waves, steps, tiles, block, info, rows, *refs):
    inv_ref, border_ref, out_ref, *wave_refs, held = refs
    step = pl.program_id(0)
    filling = steps[0]
    depth, tile = out_ref.shape[1], out_ref.shape[2]
    slot = step // tiles
    live = slot < info[2]

    def put(value):
        out_ref[0] = value
        row = pl.multiple_of(slot * depth, depth)
        column = pl.multiple_of((step % tiles) * tile, tile)
        held[pl.ds(row, depth), pl.ds(column, tile)] = value

    @pl.when((step < filling) & live)
    def _():
        inv = inv_ref[0]
        row_ids = lax.broadcasted_iota(jnp.int32, inv.shape, 0)
        inv = jnp.where(row_ids < rows[slot], inv, jnp.zeros_like(inv))
        product = jnp.dot(inv, border_ref[0], preferred_element_type=F32)
        put(product.astype(out_ref.dtype))

    @pl.when((step < filling) & jnp.logical_not(live))
    def _():
        put(jnp.zeros(out_ref.shape[1:], out_ref.dtype))

    def read(chip):
        return held[:, pl.ds(pl.multiple_of(chip * 2 * block, 2 * block), 2 * block)]

    run_products(waves, steps[1], step - filling, wave_refs, info, read, block)


def condense(info, block_rows, inv_factor, border, waves, devices, tile=1024):
    slots, rows, width = border.shape
    block = width // devices
    tile = min(tile, width)
    tiles = width // tile
    filling = slots * tiles
    products = product_steps(waves, devices // 2)

    def slot_of(step, info):
        return jnp.minimum(step // tiles, info[2] - 1)

    def source(step, info, rows_):
        live = step // tiles < info[2]
        return slot_of(step, info), 0, jnp.where(live, step % tiles, tiles - 1)

    def target(step, info, rows_):
        at = jnp.minimum(step, filling - 1)
        return at // tiles, 0, at % tiles

    shapes = wave_shapes(waves, block)
    return pl.pallas_call(
        functools.partial(condense_kernel, waves, (filling, products), tiles, block),
        out_shape=(jax.ShapeDtypeStruct(border.shape, border.dtype), *shapes),
        grid_spec=pltpu.PrefetchScalarGridSpec(
            num_scalar_prefetch=2,
            grid=(filling + len(products),),
            in_specs=[
                pl.BlockSpec(
                    (1, rows, rows), lambda s, info, rows_: (slot_of(s, info), 0, 0)
                ),
                pl.BlockSpec((1, rows, tile), source),
            ],
            out_specs=(
                pl.BlockSpec((1, rows, tile), target),
                *[whole_block(s.shape) for s in shapes],
            ),
            scratch_shapes=[pltpu.VMEM((slots * rows, width), border.dtype)],
        ),
        compiler_params=pltpu.CompilerParams(vmem_limit_bytes=32 << 20),
        cost_estimate=pl.CostEstimate(
            flops=6 * slots * rows * rows * width,
            bytes_accessed=2 * border.size * 2,
            transcendentals=0,
        ),
        name="condense",
    )(info, block_rows, inv_factor, border)


def products_kernel(waves, steps, block, info, held, *wave_refs):
    def read(chip):
        return held[:, pl.ds(pl.multiple_of(chip * 2 * block, 2 * block), 2 * block)]

    run_products(waves, steps, pl.program_id(0), wave_refs, info, read, block)


def products(info, condensed, waves, devices):
    depth, width = condensed.shape
    block = width // devices
    steps = product_steps(waves, devices // 2)
    shapes = wave_shapes(waves, block)
    return pl.pallas_call(
        functools.partial(products_kernel, waves, steps, block),
        out_shape=tuple(shapes),
        grid_spec=pltpu.PrefetchScalarGridSpec(
            num_scalar_prefetch=1,
            grid=(len(steps),),
            in_specs=[whole_block(condensed.shape)],
            out_specs=tuple(whole_block(s.shape) for s in shapes),
        ),
        compiler_params=pltpu.CompilerParams(vmem_limit_bytes=32 << 20),
        cost_estimate=pl.CostEstimate(
            flops=2 * depth * 4 * block * block * len(steps),
            bytes_accessed=condensed.size * 2,
            transcendentals=0,
        ),
        name="products",
    )(info, condensed)


def swap(x, axis, bits):
    n = lax.axis_size(axis)
    return lax.ppermute(x, axis, [(i, i ^ bits) for i in range(n)])


def after(x, *others):
    return lax.optimization_barrier((x, *others))[0]


def ordered(flip, first, second):
    return jnp.where(flip == 0, first, second), jnp.where(flip == 0, second, first)


def finish_kernel(part, chained, info, first_ref, *refs):
    refs = refs[1:] if chained else refs
    *parts, out_ref = refs
    me, flip = info[0], info[1]
    core = me & 1
    block = out_ref.shape[1]
    which = pl.program_id(0)
    own = ordered(flip, parts[0][...], parts[1][...])
    if part == DIAGONAL:
        half, quarter = block // 2, block // 4
        top = jnp.concatenate([p[:quarter] for p in own], 0)
        corner = [q for p in own for q in (p[quarter:, :half], p[quarter:, half:])]
        low = jnp.concatenate([top[:, half:].T, jnp.concatenate(corner, 0)], 1)
        out_ref[...] = first_ref[...] - jnp.concatenate([top, low], 0)
    elif part == SHARED:
        got = ordered(flip, parts[2][...], parts[3][...])
        own, got = jnp.concatenate(own, 0), jnp.concatenate(got, 0)
        whole = jnp.concatenate(
            [jnp.where(core == 0, own, got), jnp.where(core == 0, got, own)], 0
        )
        out_ref[...] = first_ref[...] - jnp.where(core == 0, whole, whole.T)
    else:
        chip = me >> 1
        high = (chip ^ part) < chip

        def put(halves):
            whole = jnp.concatenate(halves, 0)
            out_ref[...] = first_ref[...] - jnp.where(high, whole.T, whole)

        @pl.when(which == 0)
        def _():
            put(own)

        @pl.when(which == 1)
        def _():
            got = [
                jnp.where(high, a[...], b[...])
                for a, b in zip(parts[2:4], parts[4:6])
            ]
            put(ordered(flip, *got))


def finish(info, first_section, previous, parts, part):
    rows, _ = first_section.shape

    def column(k, info):
        me = info[0]
        if part == DIAGONAL:
            return 0, me
        if part == SHARED:
            return 0, me ^ 1
        chip = me >> 1
        high = ((chip ^ part) < chip).astype(jnp.int32)
        return 0, me ^ (2 * part) ^ (k ^ high)

    chained = previous is not None
    specs = [pl.BlockSpec((rows, rows), column)]
    operands = [first_section]
    if chained:
        specs.append(pl.BlockSpec(memory_space=ANY))
        operands.append(previous)
    for one in parts:
        specs.append(whole_block(one.shape))
        operands.append(one)
    return pl.pallas_call(
        functools.partial(finish_kernel, part, chained),
        out_shape=jax.ShapeDtypeStruct(first_section.shape, F32),
        grid_spec=pltpu.PrefetchScalarGridSpec(
            num_scalar_prefetch=1,
            grid=(1 if isinstance(part, str) else 2,),
            in_specs=specs,
            out_specs=pl.BlockSpec((rows, rows), column),
        ),
        input_output_aliases={2: 0} if chained else {},
        compiler_params=pltpu.CompilerParams(vmem_limit_bytes=16 << 20),
        cost_estimate=pl.CostEstimate(
            flops=rows * rows * 2, bytes_accessed=rows * rows * 32, transcendentals=0
        ),
    )(info, *operands)


def split(x, rows):
    out, at = [], 0
    for n in rows:
        out.append(x[at : at + n])
        at += n
    return out


def plan(devices):
    chips = devices // 2
    bits = list(range(1, devices.bit_length() - 1))
    axes = [*bits, "z"]
    contents = [(mu,) for mu in range(chips - 1, 0, -1)]
    turns = [k % len(axes) for k in range(len(contents))]
    waves = [(c, (*axes[k:], *axes[:k])) for c, k in zip(contents, turns)]
    waves.append(((SHARED, DIAGONAL), (bits[0], "z", *bits[1:])))
    return waves


def triangular_body(inv_factor, border, block_rows, live_count, first_section):
    slots, rows_block, width = border.shape
    devices = lax.axis_size("dev")
    groups = lax.axis_size("grp")
    block = width // devices
    info = jnp.stack(
        [
            lax.axis_index("dev").astype(jnp.int32),
            (lax.axis_index("grp") & 1).astype(jnp.int32),
            live_count[0],
        ]
    )
    waves = plan(devices)
    early, late = waves[:2], waves[2:]
    condensed, *arrays = condense(
        info, block_rows, inv_factor, border, early, devices
    )
    flat = condensed.reshape(slots * rows_block, width)

    def first_step(pair):
        kept, sent = pair
        got = swap(sent, "dev", 1)
        return kept[0] + got[0], kept[1] + got[1]

    state = [first_step(arrays[2 * k : 2 * k + 2]) for k in range(len(early))]
    arrays = products(after(info, *[s[1] for s in state]), flat, late, devices)
    state += [first_step(arrays[2 * k : 2 * k + 2]) for k in range(len(late))]

    def finish_reduction(wave, kept, send):
        parts, order = wave
        for k, step in enumerate(order):
            where = ("grp", 1) if step == "z" else ("dev", 1 << step)
            got = swap(send, *where)
            if k + 1 < len(order):
                kept, send = kept[0] + got[0], kept[1] + got[1]
        mine = kept + got
        bit = 2
        while bit < groups:
            got = swap(mine, "grp", bit)
            bit *= 2
            if bit < groups:
                mine = mine + got
        rows = heights(block, parts)
        own = [a + b for a, b in zip(split(mine, rows), split(got, rows))]
        return {p: (x, swap(x, "grp", 1)) for p, x in zip(parts, own)}

    reduced = {}
    for wave, pair in zip(waves, state):
        reduced.update(finish_reduction(wave, *pair))
    result = None
    *pairs, last = [p for parts, _ in waves[:-1] for p in parts]
    for part in (*pairs, SHARED, DIAGONAL, last):
        pieces = reduced[part]
        if part == SHARED:
            pieces = (*pieces, *[swap(x, "dev", 1) for x in pieces])
        elif part != DIAGONAL:
            direct = [swap(x, "dev", 2 * part) for x in pieces]
            pieces = (*pieces, *direct, *[swap(x, "dev", 1) for x in direct])
        result = finish(info, first_section, result, pieces, part)
    return condensed, result


def solution(mesh):
    placed = (
        P(("grp", "dev"), None, None),
        P(("grp", "dev"), None, None),
        P(("grp", "dev")),
        P(("grp", "dev")),
        P("dev", None),
    )

    def body(inv_factor, border, block_rows, live_count, first_section):
        rows, _ = first_section.shape
        devices, groups = mesh.shape["dev"], mesh.shape["grp"]
        fits = (
            power_of_two(devices)
            and devices >= 4
            and power_of_two(groups)
            and groups >= 4
            and rows % 256 == 0
            and border.shape[1] % 128 == 0
        )
        run = triangular_body if fits else plain_body
        return run(inv_factor, border, block_rows, live_count, first_section)

    return jax.shard_map(
        body,
        mesh=mesh,
        in_specs=placed,
        out_specs=(P(("grp", "dev"), None, None), P("dev", None)),
        check_vma=False,
    )
```

time: 325 us -> 127 us (0.39)
  waiting for transfers between devices: 270 us -> 47.3 us
  starting transfers between devices: 0.08 us -> 44 us
  Pallas kernels: 0 us -> 27 us
  matrix products: 20.6 us -> 0 us
  between operations: 14.1 us -> 1.46 us
  local copies, waits for them, and re-layouts: 11.4 us -> 5.27 us
  other arithmetic: 5.43 us -> 1.4 us
    reduce_scatter x1 -> x0, waiting for transfers between devices: 182 us -> none  [body(): lax.psum_scatter(accumulate(condensed, count_own, lambda piece: column_pr...]
    psum x1 -> x0, waiting for transfers between devices: 88.5 us -> none  [body(): summed = lax.psum(share, 'grp')]
    ppermute x0 -> x39, waiting for transfers between devices: none -> 47.3 us  [swap(): return lax.ppermute(x, axis, [(i, i ^ bits) for i in range(n)])]
    ppermute x0 -> x39, starting transfers between devices: none -> 44 us  [swap(): return lax.ppermute(x, axis, [(i, i ^ bits) for i in range(n)])]
    pallas_call x0 -> x7, Pallas kernels: none -> 27 us  [the longest x1 11.1 us: condense(): pl.pallas_call(functools.partial(condense_kernel, waves, (filling, produc...]
    dot_general x2 -> x0, matrix products: 20.6 us -> none  [the longest x1 17 us: column_product(): lax.dot_general(columns, piece, (((0,), (0,)), ((), ())), preferred_eleme...]
    broadcast_in_dim x2 -> x0, local copies, waits for them, and re-layouts: 11.4 us -> none  [the longest x1 7.86 us: accumulate(): jnp.zeros(out_shape, jnp.float32)]
    unnamed x2 -> x10, local copies, waits for them, and re-layouts: 0.01 us -> 5.27 us
  transfers between devices with their start and end apart: 2 -> 39, of which waited for: 2 -> 17; matrix products, arithmetic and copies ran while one was open for 0% -> 1% of each run, Pallas kernels for 0% -> 11%
where the time goes in v1:
time: 127 us
  waiting for transfers between devices  47.3 us (37%)
  starting transfers between devices  44 us (35%)
  Pallas kernels  27 us (21%)
  local copies, waits for them, and re-layouts  5.27 us (4%)
  between operations  1.46 us (1%)
  other arithmetic  1.4 us (1%)
    ppermute x39, waiting for transfers between devices, swap(): return lax.ppermute(x, axis, [(i, i ^ bits) for i in range(n)])  47.3 us
    ppermute x39, starting transfers between devices, swap(): return lax.ppermute(x, axis, [(i, i ^ bits) for i in range(n)])  44 us
    pallas_call x1, Pallas kernels, condense(): pl.pallas_call(functools.partial(condense_kernel, waves, (filling, produc...  11.1 us
    pallas_call x1, Pallas kernels, products(): pl.pallas_call(functools.partial(products_kernel, waves, steps, block), o...  8.05 us
    pallas_call x5, Pallas kernels, finish(): pl.pallas_call(functools.partial(finish_kernel, part, chained), out_shape...  7.82 us
    unnamed x10, local copies, waits for them, and re-layouts  5.27 us
  transfers between devices with their start and end apart: 39, of which 17 were waited for; matrix products, arithmetic and copies ran while one was open for 1% of the time, Pallas kernels for 11%

profile of v1, /device:TPU:0, one launch (start us, length us, event | category | flops | bytes accessed | tf_op | source)
XLA Modules:
  0.0 126.5 jit_solution(6352994350731376674)
XLA Ops:
  1.4 2.8 %copy-done.1 = bf16[4,384,2048]{2,1,0:T(8,128)(2,1)S(1)} copy-done((bf16[4,384,2048]{2,1,0:T(8,128)(2,1)S(1)}, bf16[4,384,2048]{2,1,0:T(8,128)(2,1)}, u32[]{:S(2)}) %copy-start.1) | copy-done | bytes 6291480
  6.1 11.1 %condense.1 = (bf16[4,384,2048]{2,1,0:T(8,128)(2,1)}, f32[2,2,2,128,256]{4,3,2,1,0:T(8,128)S(1)}, f32[2,2,2,128,256]{4,3,2,1,0:T(8,128)S(1)}, f32[2,2,2,128,256]...) custom-call(s32[3]{0:T(128)S(1)} %pad_add_fusion.info, s32[4]{0:T(128)S(1)} %copy-done.3, bf16[4,384,384]{2,1,0:T(8,128)(2,1)S(1)} %copy-done.2, ...), custom_call_target="tpu_custom_call" | custom-call | flops 7247757312 | bytes 12582912 | tf_op jit(solution)/shard_map/condense/pallas_call | solution.py:198
  17.2 2.2 %collective-permute-start = (f32[2,2,2,128,256]{4,3,2,1,0:T(8,128)S(1)}, f32[2,2,2,128,256]{4,3,2,1,0:T(8,128)S(1)}, u32[]{:S(2)}, u32[]{:S(2)}) collective-permute-start(f32[2,2,2,128,256]{4,3,2,1,0:T(8,128)S(1)} %get-tuple-element.14), channel_id=1, source_target_pairs={{0,1},{1,0},{2,3},{3,2},{4,5},{5,4},{6,7},{7,6},{8,9},{9,8},{10,11... | collective-permute-start | bytes 3145736 | tf_op jit(solution)/shard_map/ppermute | solution.py:259
  19.4 2.3 %collective-permute-done = f32[2,2,2,128,256]{4,3,2,1,0:T(8,128)S(1)} collective-permute-done((f32[2,2,2,128,256]{4,3,2,1,0:T(8,128)S(1)}, f32[2,2,2,128,256]{4,3,2,1,0:T(8,128)S(1)}, u32[]{:S(2)}, u32[]{:S(2)}) %collective-permute-start) | collective-permute-done | bytes 1048608 | tf_op jit(solution)/shard_map/ppermute | solution.py:259
  21.8 1.8 %collective-permute-start.1 = (f32[2,2,128,256]{3,2,1,0:T(8,128)S(1)}, f32[2,2,128,256]{3,2,1,0:T(8,128)S(1)}, u32[]{:S(2)}, u32[]{:S(2)}) collective-permute-start(f32[2,2,128,256]{3,2,1,0:T(8,128)S(1)} %get-tuple-element.29), channel_id=1, source_target_pairs={{0,2},{1,3},{2,0},{3,1},{4,6},{5,7},{6,4},{7,5},{8,10},{9,11},{10,... | collective-permute-start | bytes 1572872 | tf_op jit(solution)/shard_map/ppermute | solution.py:259
  24.4 8.1 %products.1 = (f32[2,2,2,128,256]{4,3,2,1,0:T(8,128)S(1)}, f32[2,2,2,128,256]{4,3,2,1,0:T(8,128)S(1)}, f32[2,2,2,160,256]{4,3,2,1,0:T(8,128)S(1)}, f32[2,2,2,160,256]{4,3,2,1,0:T(8,128)S(1)}) custom-call(s32[3]{0:T(128)S(1)} %pad_add_fusion.info, bf16[1536,2048]{1,0:T(8,128)(2,1)S(1)} %bitcast.107), custom_call_target="tpu_custom_call" | custom-call | flops 4831838208 | bytes 6291456 | tf_op jit(solution)/shard_map/products/pallas_call | solution.py:238
  33.1 1.8 %collective-permute-start.11 = (f32[2,2,128,256]{3,2,1,0:T(8,128)S(1)}, f32[2,2,128,256]{3,2,1,0:T(8,128)S(1)}, u32[]{:S(2)}, u32[]{:S(2)}) collective-permute-start(f32[2,2,128,256]{3,2,1,0:T(8,128)S(1)} %get-tuple-element.27), channel_id=1, source_target_pairs={{0,4},{1,5},{2,6},{3,7},{4,0},{5,1},{6,2},{7,3},{8,12},{9,13},{10,... | collective-permute-start | bytes 1572872 | tf_op jit(solution)/shard_map/ppermute | solution.py:259
  36.2 1.8 %collective-permute-start.2 = (f32[2,128,256]{2,1,0:T(8,128)S(1)}, f32[2,128,256]{2,1,0:T(8,128)S(1)}, u32[]{:S(2)}, u32[]{:S(2)}) collective-permute-start(f32[2,128,256]{2,1,0:T(8,128)S(1)} %get-tuple-element.37), channel_id=1, source_target_pairs={{0,4},{1,5},{2,6},{3,7},{4,0},{5,1},{6,2},{7,3},{8,12},{9,13},{10,... | collective-permute-start | bytes 786440 | tf_op jit(solution)/shard_map/ppermute | solution.py:259
  38.0 9.8 %collective-permute-done.11 = f32[2,2,128,256]{3,2,1,0:T(8,128)S(1)} collective-permute-done((f32[2,2,128,256]{3,2,1,0:T(8,128)S(1)}, f32[2,2,128,256]{3,2,1,0:T(8,128)S(1)}, u32[]{:S(2)}, u32[]{:S(2)}) %collective-permute-start.11) | collective-permute-done | bytes 524320 | tf_op jit(solution)/shard_map/ppermute | solution.py:259
  47.9 2.5 %collective-permute-start.12 = (f32[2,128,256]{2,1,0:T(8,128)S(1)}, f32[2,128,256]{2,1,0:T(8,128)S(1)}, u32[]{:S(2)}, u32[]{:S(2)}) collective-permute-start(f32[2,128,256]{2,1,0:T(8,128)S(1)} %get-tuple-element.35), channel_id=1, source_target_pairs={{0,8},{8,0},{16,24},{24,16},{1,9},{9,1},{17,25},{25,17},{2,10},{10... | collective-permute-start | bytes 786440 | tf_op jit(solution)/shard_map/ppermute | solution.py:259
  50.4 2.6 %collective-permute-done.2 = f32[2,128,256]{2,1,0:T(8,128)S(1)} collective-permute-done((f32[2,128,256]{2,1,0:T(8,128)S(1)}, f32[2,128,256]{2,1,0:T(8,128)S(1)}, u32[]{:S(2)}, u32[]{:S(2)}) %collective-permute-start.2) | collective-permute-done | bytes 262176 | tf_op jit(solution)/shard_map/ppermute | solution.py:259
  53.0 2.4 %collective-permute-start.3 = (f32[128,256]{1,0:T(8,128)S(1)}, f32[128,256]{1,0:T(8,128)S(1)}, u32[]{:S(2)}, u32[]{:S(2)}) collective-permute-start(f32[128,256]{1,0:T(8,128)S(1)} %fusion.17), channel_id=1, source_target_pairs={{0,8},{8,0},{16,24},{24,16},{1,9},{9,1},{17,25},{25,17},{2,10},{10... | collective-permute-start | bytes 393224 | tf_op jit(solution)/shard_map/ppermute | solution.py:259
  59.8 2.8 %collective-permute-start.4 = (f32[128,256]{1,0:T(8,128)S(1)}, f32[128,256]{1,0:T(8,128)S(1)}, u32[]{:S(2)}, u32[]{:S(2)}) collective-permute-start(f32[128,256]{1,0:T(8,128)S(1)} %fusion.19), channel_id=1, source_target_pairs={{0,16},{8,24},{16,0},{24,8},{1,17},{9,25},{17,1},{25,9},{2,18},{10... | collective-permute-start | bytes 393224 | tf_op jit(solution)/shard_map/ppermute | solution.py:259
  62.6 10.2 %collective-permute-done.30 = f32[2,2,128,256]{3,2,1,0:T(8,128)S(1)} collective-permute-done((f32[2,2,128,256]{3,2,1,0:T(8,128)S(1)}, f32[2,2,128,256]{3,2,1,0:T(8,128)S(1)}, u32[]{:S(2)}, u32[]{:S(2)}) %collective-permute-start.30) | collective-permute-done | bytes 524320 | tf_op jit(solution)/shard_map/ppermute | solution.py:259
  75.8 2.8 %collective-permute-start.14 = (f32[128,256]{1,0:T(8,128)S(1)}, f32[128,256]{1,0:T(8,128)S(1)}, u32[]{:S(2)}, u32[]{:S(2)}) collective-permute-start(f32[128,256]{1,0:T(8,128)S(1)} %fusion.16), channel_id=1, source_target_pairs={{0,16},{8,24},{16,0},{24,8},{1,17},{9,25},{17,1},{25,9},{2,18},{10... | collective-permute-start | bytes 393224 | tf_op jit(solution)/shard_map/ppermute | solution.py:259
  78.6 2.8 %collective-permute-start.6 = (f32[128,256]{1,0:T(8,128)S(1)}, f32[128,256]{1,0:T(8,128)S(1)}, u32[]{:S(2)}, u32[]{:S(2)}) collective-permute-start(f32[128,256]{1,0:T(8,128)S(1)} %add.166.refs_0_), channel_id=1, source_target_pairs={{0,6},{1,7},{2,4},{3,5},{4,2},{5,3},{6,0},{7,1},{8,14},{9,15},{10,... | collective-permute-start | bytes 393224 | tf_op jit(solution)/shard_map/ppermute | solution.py:259
  83.3 3.1 %collective-permute-done.22 = f32[2,160,256]{2,1,0:T(8,128)S(1)} collective-permute-done((f32[2,160,256]{2,1,0:T(8,128)S(1)}, f32[2,160,256]{2,1,0:T(8,128)S(1)}, u32[]{:S(2)}, u32[]{:S(2)}) %collective-permute-start.22) | collective-permute-done | bytes 327712 | tf_op jit(solution)/shard_map/ppermute | solution.py:259
  87.5 2.8 %collective-permute-start.33 = (f32[128,256]{1,0:T(8,128)S(1)}, f32[128,256]{1,0:T(8,128)S(1)}, u32[]{:S(2)}, u32[]{:S(2)}) collective-permute-start(f32[128,256]{1,0:T(8,128)S(1)} %fusion.13), channel_id=1, source_target_pairs={{0,16},{8,24},{16,0},{24,8},{1,17},{9,25},{17,1},{25,9},{2,18},{10... | collective-permute-start | bytes 393224 | tf_op jit(solution)/shard_map/ppermute | solution.py:259
  94.0 2.6 %collective-permute-start.15 = (f32[128,256]{1,0:T(8,128)S(1)}, f32[128,256]{1,0:T(8,128)S(1)}, u32[]{:S(2)}, u32[]{:S(2)}) collective-permute-start(f32[128,256]{1,0:T(8,128)S(1)} %add.178.refs_1_), channel_id=1, source_target_pairs={{0,8},{8,0},{16,24},{24,16},{1,9},{9,1},{17,25},{25,17},{2,10},{10... | collective-permute-start | bytes 393224 | tf_op jit(solution)/shard_map/ppermute | solution.py:259
  96.6 3.3 %collective-permute-done.33 = f32[128,256]{1,0:T(8,128)S(1)} collective-permute-done((f32[128,256]{1,0:T(8,128)S(1)}, f32[128,256]{1,0:T(8,128)S(1)}, u32[]{:S(2)}, u32[]{:S(2)}) %collective-permute-start.33) | collective-permute-done | bytes 131104 | tf_op jit(solution)/shard_map/ppermute | solution.py:259
  100.0 2.4 %collective-permute-start.7 = (f32[128,256]{1,0:T(8,128)S(1)}, f32[128,256]{1,0:T(8,128)S(1)}, u32[]{:S(2)}, u32[]{:S(2)}) collective-permute-start(f32[128,256]{1,0:T(8,128)S(1)} %collective-permute-done.5.refs_1_), channel_id=1, source_target_pairs={{0,6},{1,7},{2,4},{3,5},{4,2},{5,3},{6,0},{7,1},{8,14},{9,15},{10,... | collective-permute-start | bytes 393224 | tf_op jit(solution)/shard_map/ppermute | solution.py:259
  103.2 2.6 %collective-permute-done.34.refs_2_ = f32[128,256]{1,0:T(8,128)S(1)} collective-permute-done((f32[128,256]{1,0:T(8,128)S(1)}, f32[128,256]{1,0:T(8,128)S(1)}, u32[]{:S(2)}, u32[]{:S(2)}) %collective-permute-start.34) | collective-permute-done | bytes 131104 | tf_op jit(solution)/shard_map/ppermute | solution.py:259
  109.7 2.5 %collective-permute-done.35.refs_3_ = f32[128,256]{1,0:T(8,128)S(1)} collective-permute-done((f32[128,256]{1,0:T(8,128)S(1)}, f32[128,256]{1,0:T(8,128)S(1)}, u32[]{:S(2)}, u32[]{:S(2)}) %collective-permute-start.35) | collective-permute-done | bytes 131104 | tf_op jit(solution)/shard_map/ppermute | solution.py:259
  115.8 2.8 %collective-permute-done.25.refs_2_ = f32[64,256]{1,0:T(8,128)S(1)} collective-permute-done((f32[64,256]{1,0:T(8,128)S(1)}, f32[64,256]{1,0:T(8,128)S(1)}, u32[]{:S(2)}, u32[]{:S(2)}) %collective-permute-start.25) | collective-permute-done | bytes 65568 | tf_op jit(solution)/shard_map/ppermute | solution.py:259
  (93 shorter events, 35.2 us)
Async XLA Ops:
  21.8 14.3 %collective-permute-start.1 = (f32[2,2,128,256]{3,2,1,0:T(8,128)S(1)}, f32[2,2,128,256]{3,2,1,0:T(8,128)S(1)}, u32[]{:S(2)}, u32[]{:S(2)}) collective-permute-start(f32[2,2,128,256]{3,2,1,0:T(8,128)S(1)} %get-tuple-element.29), channel_id=1, source_target_pairs={{0,2},{1,3},{2,0},{3,1},{4,6},{5,7},{6,4},{7,5},{8,10},{9,11},{10,... | collective-permute-start | bytes 1572872 | tf_op jit(solution)/shard_map/ppermute | solution.py:259
  32.5 22.9 %collective-permute-start.29 = (f32[2,2,2,128,256]{4,3,2,1,0:T(8,128)S(1)}, f32[2,2,2,128,256]{4,3,2,1,0:T(8,128)S(1)}, u32[]{:S(2)}, u32[]{:S(2)}) collective-permute-start(f32[2,2,2,128,256]{4,3,2,1,0:T(8,128)S(1)} %get-tuple-element.21), channel_id=1, source_target_pairs={{0,1},{1,0},{2,3},{3,2},{4,5},{5,4},{6,7},{7,6},{8,9},{9,8},{10,11... | collective-permute-start | bytes 3145736 | tf_op jit(solution)/shard_map/ppermute | solution.py:259
  33.0 22.7 %collective-permute-start.20 = (f32[2,2,2,160,256]{4,3,2,1,0:T(8,128)S(1)}, f32[2,2,2,160,256]{4,3,2,1,0:T(8,128)S(1)}, u32[]{:S(2)}, u32[]{:S(2)}) collective-permute-start(f32[2,2,2,160,256]{4,3,2,1,0:T(8,128)S(1)} %get-tuple-element.19), channel_id=1, source_target_pairs={{0,1},{1,0},{2,3},{3,2},{4,5},{5,4},{6,7},{7,6},{8,9},{9,8},{10,11... | collective-permute-start | bytes 3932168 | tf_op jit(solution)/shard_map/ppermute | solution.py:259
  33.1 14.8 %collective-permute-start.11 = (f32[2,2,128,256]{3,2,1,0:T(8,128)S(1)}, f32[2,2,128,256]{3,2,1,0:T(8,128)S(1)}, u32[]{:S(2)}, u32[]{:S(2)}) collective-permute-start(f32[2,2,128,256]{3,2,1,0:T(8,128)S(1)} %get-tuple-element.27), channel_id=1, source_target_pairs={{0,4},{1,5},{2,6},{3,7},{4,0},{5,1},{6,2},{7,3},{8,12},{9,13},{10,... | collective-permute-start | bytes 1572872 | tf_op jit(solution)/shard_map/ppermute | solution.py:259
  36.2 16.8 %collective-permute-start.2 = (f32[2,128,256]{2,1,0:T(8,128)S(1)}, f32[2,128,256]{2,1,0:T(8,128)S(1)}, u32[]{:S(2)}, u32[]{:S(2)}) collective-permute-start(f32[2,128,256]{2,1,0:T(8,128)S(1)} %get-tuple-element.37), channel_id=1, source_target_pairs={{0,4},{1,5},{2,6},{3,7},{4,0},{5,1},{6,2},{7,3},{8,12},{9,13},{10,... | collective-permute-start | bytes 786440 | tf_op jit(solution)/shard_map/ppermute | solution.py:259
  47.9 9.4 %collective-permute-start.12 = (f32[2,128,256]{2,1,0:T(8,128)S(1)}, f32[2,128,256]{2,1,0:T(8,128)S(1)}, u32[]{:S(2)}, u32[]{:S(2)}) collective-permute-start(f32[2,128,256]{2,1,0:T(8,128)S(1)} %get-tuple-element.35), channel_id=1, source_target_pairs={{0,8},{8,0},{16,24},{24,16},{1,9},{9,1},{17,25},{25,17},{2,10},{10... | collective-permute-start | bytes 786440 | tf_op jit(solution)/shard_map/ppermute | solution.py:259
  55.6 17.2 %collective-permute-start.30 = (f32[2,2,128,256]{3,2,1,0:T(8,128)S(1)}, f32[2,2,128,256]{3,2,1,0:T(8,128)S(1)}, u32[]{:S(2)}, u32[]{:S(2)}) collective-permute-start(f32[2,2,128,256]{3,2,1,0:T(8,128)S(1)} %get-tuple-element.25), channel_id=1, source_target_pairs={{0,8},{8,0},{16,24},{24,16},{1,9},{9,1},{17,25},{25,17},{2,10},{10... | collective-permute-start | bytes 1572872 | tf_op jit(solution)/shard_map/ppermute | solution.py:259
  55.9 18.0 %collective-permute-start.21 = (f32[2,2,160,256]{3,2,1,0:T(8,128)S(1)}, f32[2,2,160,256]{3,2,1,0:T(8,128)S(1)}, u32[]{:S(2)}, u32[]{:S(2)}) collective-permute-start(f32[2,2,160,256]{3,2,1,0:T(8,128)S(1)} %get-tuple-element.23), channel_id=1, source_target_pairs={{0,2},{1,3},{2,0},{3,1},{4,6},{5,7},{6,4},{7,5},{8,10},{9,11},{10,... | collective-permute-start | bytes 1966088 | tf_op jit(solution)/shard_map/ppermute | solution.py:259
  57.4 18.4 %collective-permute-start.13 = (f32[128,256]{1,0:T(8,128)S(1)}, f32[128,256]{1,0:T(8,128)S(1)}, u32[]{:S(2)}, u32[]{:S(2)}) collective-permute-start(f32[128,256]{1,0:T(8,128)S(1)} %fusion.14), channel_id=1, source_target_pairs={{0,2},{1,3},{2,0},{3,1},{4,6},{5,7},{6,4},{7,5},{8,10},{9,11},{10,... | collective-permute-start | bytes 393224 | tf_op jit(solution)/shard_map/ppermute | solution.py:259
  59.8 18.8 %collective-permute-start.4 = (f32[128,256]{1,0:T(8,128)S(1)}, f32[128,256]{1,0:T(8,128)S(1)}, u32[]{:S(2)}, u32[]{:S(2)}) collective-permute-start(f32[128,256]{1,0:T(8,128)S(1)} %fusion.19), channel_id=1, source_target_pairs={{0,16},{8,24},{16,0},{24,8},{1,17},{9,25},{17,1},{25,9},{2,18},{10... | collective-permute-start | bytes 393224 | tf_op jit(solution)/shard_map/ppermute | solution.py:259
  72.8 8.9 %collective-permute-start.31 = (f32[2,128,256]{2,1,0:T(8,128)S(1)}, f32[2,128,256]{2,1,0:T(8,128)S(1)}, u32[]{:S(2)}, u32[]{:S(2)}) collective-permute-start(f32[2,128,256]{2,1,0:T(8,128)S(1)} %get-tuple-element.33), channel_id=1, source_target_pairs={{0,2},{1,3},{2,0},{3,1},{4,6},{5,7},{6,4},{7,5},{8,10},{9,11},{10,... | collective-permute-start | bytes 786440 | tf_op jit(solution)/shard_map/ppermute | solution.py:259
  74.1 12.4 %collective-permute-start.22 = (f32[2,160,256]{2,1,0:T(8,128)S(1)}, f32[2,160,256]{2,1,0:T(8,128)S(1)}, u32[]{:S(2)}, u32[]{:S(2)}) collective-permute-start(f32[2,160,256]{2,1,0:T(8,128)S(1)} %get-tuple-element.31), channel_id=1, source_target_pairs={{0,8},{8,0},{16,24},{24,16},{1,9},{9,1},{17,25},{25,17},{2,10},{10... | collective-permute-start | bytes 983048 | tf_op jit(solution)/shard_map/ppermute | solution.py:259
  75.8 16.6 %collective-permute-start.14 = (f32[128,256]{1,0:T(8,128)S(1)}, f32[128,256]{1,0:T(8,128)S(1)}, u32[]{:S(2)}, u32[]{:S(2)}) collective-permute-start(f32[128,256]{1,0:T(8,128)S(1)} %fusion.16), channel_id=1, source_target_pairs={{0,16},{8,24},{16,0},{24,8},{1,17},{9,25},{17,1},{25,9},{2,18},{10... | collective-permute-start | bytes 393224 | tf_op jit(solution)/shard_map/ppermute | solution.py:259
  78.6 15.4 %collective-permute-start.6 = (f32[128,256]{1,0:T(8,128)S(1)}, f32[128,256]{1,0:T(8,128)S(1)}, u32[]{:S(2)}, u32[]{:S(2)}) collective-permute-start(f32[128,256]{1,0:T(8,128)S(1)} %add.166.refs_0_), channel_id=1, source_target_pairs={{0,6},{1,7},{2,4},{3,5},{4,2},{5,3},{6,0},{7,1},{8,14},{9,15},{10,... | collective-permute-start | bytes 393224 | tf_op jit(solution)/shard_map/ppermute | solution.py:259
  81.5 18.4 %collective-permute-start.5 = (f32[128,256]{1,0:T(8,128)S(1)}, f32[128,256]{1,0:T(8,128)S(1)}, u32[]{:S(2)}, u32[]{:S(2)}) collective-permute-start(f32[128,256]{1,0:T(8,128)S(1)} %add.166.refs_0_), channel_id=1, source_target_pairs={{0,8},{8,0},{16,24},{24,16},{1,9},{9,1},{17,25},{25,17},{2,10},{10... | collective-permute-start | bytes 393224 | tf_op jit(solution)/shard_map/ppermute | solution.py:259
  87.5 12.3 %collective-permute-start.33 = (f32[128,256]{1,0:T(8,128)S(1)}, f32[128,256]{1,0:T(8,128)S(1)}, u32[]{:S(2)}, u32[]{:S(2)}) collective-permute-start(f32[128,256]{1,0:T(8,128)S(1)} %fusion.13), channel_id=1, source_target_pairs={{0,16},{8,24},{16,0},{24,8},{1,17},{9,25},{17,1},{25,9},{2,18},{10... | collective-permute-start | bytes 393224 | tf_op jit(solution)/shard_map/ppermute | solution.py:259
  91.9 15.2 %collective-permute-start.24 = (f32[160,256]{1,0:T(8,128)S(1)}, f32[160,256]{1,0:T(8,128)S(1)}, u32[]{:S(2)}, u32[]{:S(2)}) collective-permute-start(f32[160,256]{1,0:T(8,128)S(1)} %fusion.10), channel_id=1, source_target_pairs={{0,16},{8,24},{16,0},{24,8},{1,17},{9,25},{17,1},{25,9},{2,18},{10... | collective-permute-start | bytes 491528 | tf_op jit(solution)/shard_map/ppermute | solution.py:259
  92.4 7.5 %collective-permute-start.16 = (f32[128,256]{1,0:T(8,128)S(1)}, f32[128,256]{1,0:T(8,128)S(1)}, u32[]{:S(2)}, u32[]{:S(2)}) collective-permute-start(f32[128,256]{1,0:T(8,128)S(1)} %add.178.refs_1_), channel_id=1, source_target_pairs={{0,4},{1,5},{2,6},{3,7},{4,0},{5,1},{6,2},{7,3},{8,12},{9,13},{10,... | collective-permute-start | bytes 393224 | tf_op jit(solution)/shard_map/ppermute | solution.py:259
  94.0 8.5 %collective-permute-start.15 = (f32[128,256]{1,0:T(8,128)S(1)}, f32[128,256]{1,0:T(8,128)S(1)}, u32[]{:S(2)}, u32[]{:S(2)}) collective-permute-start(f32[128,256]{1,0:T(8,128)S(1)} %add.178.refs_1_), channel_id=1, source_target_pairs={{0,8},{8,0},{16,24},{24,16},{1,9},{9,1},{17,25},{25,17},{2,10},{10... | collective-permute-start | bytes 393224 | tf_op jit(solution)/shard_map/ppermute | solution.py:259
  100.0 7.9 %collective-permute-start.7 = (f32[128,256]{1,0:T(8,128)S(1)}, f32[128,256]{1,0:T(8,128)S(1)}, u32[]{:S(2)}, u32[]{:S(2)}) collective-permute-start(f32[128,256]{1,0:T(8,128)S(1)} %collective-permute-done.5.refs_1_), channel_id=1, source_target_pairs={{0,6},{1,7},{2,4},{3,5},{4,2},{5,3},{6,0},{7,1},{8,14},{9,15},{10,... | collective-permute-start | bytes 393224 | tf_op jit(solution)/shard_map/ppermute | solution.py:259
  102.5 11.2 %collective-permute-start.18 = (f32[128,256]{1,0:T(8,128)S(1)}, f32[128,256]{1,0:T(8,128)S(1)}, u32[]{:S(2)}, u32[]{:S(2)}) collective-permute-start(f32[128,256]{1,0:T(8,128)S(1)} %collective-permute-done.16.refs_3_), channel_id=1, source_target_pairs={{0,1},{1,0},{2,3},{3,2},{4,5},{5,4},{6,7},{7,6},{8,9},{9,8},{10,11... | collective-permute-start | bytes 393224 | tf_op jit(solution)/shard_map/ppermute | solution.py:259
  112.2 12.6 %collective-permute-start.37 = (f32[128,256]{1,0:T(8,128)S(1)}, f32[128,256]{1,0:T(8,128)S(1)}, u32[]{:S(2)}, u32[]{:S(2)}) collective-permute-start(f32[128,256]{1,0:T(8,128)S(1)} %collective-permute-done.35.refs_3_), channel_id=1, source_target_pairs={{0,1},{1,0},{2,3},{3,2},{4,5},{5,4},{6,7},{7,6},{8,9},{9,8},{10,11... | collective-permute-start | bytes 393224 | tf_op jit(solution)/shard_map/ppermute | solution.py:259
  113.7 11.1 %collective-permute-start.38 = (f32[128,256]{1,0:T(8,128)S(1)}, f32[128,256]{1,0:T(8,128)S(1)}, u32[]{:S(2)}, u32[]{:S(2)}) collective-permute-start(f32[128,256]{1,0:T(8,128)S(1)} %collective-permute-done.36.refs_4_), channel_id=1, source_target_pairs={{0,1},{1,0},{2,3},{3,2},{4,5},{5,4},{6,7},{7,6},{8,9},{9,8},{10,11... | collective-permute-start | bytes 393224 | tf_op jit(solution)/shard_map/ppermute | solution.py:259
  114.3 9.2 %collective-permute-start.28 = (f32[96,256]{1,0:T(8,128)S(1)}, f32[96,256]{1,0:T(8,128)S(1)}, u32[]{:S(2)}, u32[]{:S(2)}) collective-permute-start(f32[96,256]{1,0:T(8,128)S(1)} %slice_add_fusion.24.refs_1_), channel_id=1, source_target_pairs={{0,8},{8,0},{16,24},{24,16},{1,9},{9,1},{17,25},{25,17},{2,10},{10... | collective-permute-start | bytes 294920 | tf_op jit(solution)/shard_map/ppermute | solution.py:259
  (20 other events, 134.8 us)
